TPU v7x, 32 devices: a whole 2x2x4 slice. The times are simulated.
32 devices in a mesh: dp: 4 (over x, core), shard: 8 (over z, y).
Axes of the slice: x: 2, y: 2, z: 4, core: 2. Of those that a mesh axis runs over, the one named last changes fastest.
Arguments:
- tokens: bfloat16 [256, 6144], P('dp', 'shard'), may hold values from -6 to 6
- cotangent: bfloat16 [256, 6144], P('dp', 'shard'), may hold values from -12 to 12
- gate_proj: bfloat16 [2, 6144, 16384], P(None, 'dp', 'shard'), may hold values from -0.078125 to 0.078125
- up_proj: bfloat16 [2, 6144, 16384], P(None, 'dp', 'shard'), may hold values from -0.078125 to 0.078125
- down_proj: bfloat16 [2, 16384, 6144], P(None, 'shard', 'dp'), may hold values from -0.046875 to 0.046875
- slot_tokens: int32 [2, 64], P(None, 'dp'), may hold values from 0 to 63, as said below
- gate_weights: float32 [2, 64], P(None, 'dp'), may hold values from 0.1 to 1
- live_counts: int32 [2, 4], P(None, 'dp'), may hold values from 1 to 16, as said below
Outputs:
- grad_tokens: bfloat16 [256, 6144], P('dp', 'shard')
- grad_gate_proj: bfloat16 [2, 6144, 16384], P(None, 'dp', 'shard')
- grad_up_proj: bfloat16 [2, 6144, 16384], P(None, 'dp', 'shard')
- grad_down_proj: bfloat16 [2, 16384, 6144], P(None, 'shard', 'dp')
Inputs may be any that keep to these rules, and one draw needn't show every extreme that they name: `slot_tokens`: for each expert and each index of dp, the 16 slots name 16 different tokens of that index. `live_counts`: the live slots of an expert at an index of dp are its first ones; 16 is reached at some index of every expert.
All inputs are finite; a program needn't handle non-finite values.
Results may differ from a plain program's by a relative error of at most 0.03.
Values may be sent and summed in bfloat16 or wider, within the bound.
A program may use at most 128 MiB of HBM per device.

v0:
```python
import jax
import jax.numpy as jnp
from jax import lax
from jax.sharding import PartitionSpec as P


def slope_terms(gate_sum, up_sum, cot_hidden):
    sigmoid_part = jax.nn.sigmoid(gate_sum)
    grad_gate = (
        cot_hidden * up_sum * sigmoid_part * (1.0 + gate_sum * (1.0 - sigmoid_part))
    ).astype(jnp.bfloat16)
    grad_up = (cot_hidden * gate_sum * sigmoid_part).astype(jnp.bfloat16)
    return (grad_gate, grad_up)


def on_device(
    tokens, cotangent, gate_proj, up_proj, down_proj, slot_tokens, gate_weights, live_counts
):
    experts_here = slot_tokens.shape[0]
    slot_count = slot_tokens.shape[1]
    token_count = tokens.shape[0]
    position = lax.broadcasted_iota(jnp.int32, slot_tokens.shape, 1)
    alive_mask = (position < live_counts).astype(jnp.float32)
    picked = tokens[slot_tokens]
    weighted = (
        cotangent[slot_tokens].astype(jnp.float32) * (gate_weights * alive_mask)[:, :, None]
    ).astype(jnp.bfloat16)
    full_rows, full_cot = (
        lax.all_gather(picked, "shard", axis=2, tiled=True),
        lax.all_gather(weighted, "shard", axis=2, tiled=True),
    )
    block_rows, block_cot = (
        lax.all_to_all(full_rows, "dp", split_axis=2, concat_axis=1, tiled=True),
        lax.all_to_all(full_cot, "dp", split_axis=2, concat_axis=1, tiled=True),
    )
    totals = lax.psum(live_counts, "dp").astype(jnp.float32)
    gate_part = jnp.einsum(
        "erd,edf->erf", block_rows, gate_proj, preferred_element_type=jnp.float32
    )
    up_part = jnp.einsum("erd,edf->erf", block_rows, up_proj, preferred_element_type=jnp.float32)
    cot_part = jnp.einsum("erd,efd->erf", block_cot, down_proj, preferred_element_type=jnp.float32)
    gate_total, up_total = (
        lax.psum(gate_part.astype(jnp.bfloat16), "dp").astype(jnp.float32),
        lax.psum(up_part.astype(jnp.bfloat16), "dp").astype(jnp.float32),
    )
    hidden_all = (jax.nn.silu(gate_total) * up_total).astype(jnp.bfloat16)
    cot_total = lax.psum(cot_part.astype(jnp.bfloat16), "dp").astype(jnp.float32)
    gate_all, up_all = slope_terms(gate_total, up_total, cot_total)
    scale_back = totals[:, :, None]
    grad_down_proj = (
        jnp.einsum("erf,erd->efd", hidden_all, block_cot, preferred_element_type=jnp.float32)
        / scale_back
    ).astype(jnp.bfloat16)
    grad_gate_proj = (
        jnp.einsum("erd,erf->edf", block_rows, gate_all, preferred_element_type=jnp.float32)
        / scale_back
    ).astype(jnp.bfloat16)
    grad_up_proj = (
        jnp.einsum("erd,erf->edf", block_rows, up_all, preferred_element_type=jnp.float32)
        / scale_back
    ).astype(jnp.bfloat16)
    back_term = (
        jnp.einsum("erf,edf->erd", gate_all, gate_proj, preferred_element_type=jnp.float32)
        + jnp.einsum("erf,edf->erd", up_all, up_proj, preferred_element_type=jnp.float32)
    ).astype(jnp.bfloat16)
    owned_rows = lax.all_to_all(back_term, "dp", split_axis=1, concat_axis=2, tiled=True)
    row_grads = lax.psum_scatter(
        owned_rows.astype(jnp.float32).astype(jnp.bfloat16),
        "shard",
        scatter_dimension=2,
        tiled=True,
    ).astype(jnp.float32)
    one_hot = (
        slot_tokens[:, :, None]
        == lax.broadcasted_iota(jnp.int32, (experts_here, slot_count, token_count), 2)
    ).astype(jnp.float32)
    grad_tokens = jnp.einsum("ert,erf->tf", one_hot, row_grads).astype(jnp.bfloat16)
    return (grad_tokens, grad_gate_proj, grad_up_proj, grad_down_proj)


def solution(mesh):
    in_specs = (
        P("dp", "shard"),
        P("dp", "shard"),
        P(None, "dp", "shard"),
        P(None, "dp", "shard"),
        P(None, "shard", "dp"),
        P(None, "dp"),
        P(None, "dp"),
        P(None, "dp"),
    )
    out_specs = (
        P("dp", "shard"),
        P(None, "dp", "shard"),
        P(None, "dp", "shard"),
        P(None, "shard", "dp"),
    )
    return jax.shard_map(
        on_device, mesh=mesh, in_specs=in_specs, out_specs=out_specs, check_vma=False
    )
```

profile of v0, /device:TPU:3, one launch (start us, length us, event | category | flops | bytes accessed | tf_op | source)
XLA Modules:
  0.0 304.2 jit_solution(18017264233754935161)
XLA Ops:
  7.2 0.0 copy-start
  7.2 0.7 compare_select_fusion
  7.9 0.1 reshape.13
  8.0 0.1 copy-done
  8.1 0.6 gather_fusion.1
  8.7 27.0 %all-gather = bf16[2,16,6144]{2,1,0:T(8,128)(2,1)} all-gather(bf16[2,16,768]{2,1,0:T(8,128)(2,1)S(1)} %bitcast.48), channel_id=2, replica_groups=mesh['dp'=4,'shard'=8] {'shard'}, dimensions={2}, use_global_device_ids=true | all-gather | bytes 442368 | tf_op jit(solution)/shard_map/all_gather | solution.py:29
  35.7 6.1 %copy.27 = bf16[2,16,6144]{1,0,2:T(2,128)(2,1)S(1)} copy(bf16[2,16,6144]{2,1,0:T(8,128)(2,1)} %all-gather) | data formatting | bytes 786432 | tf_op jit(solution)/shard_map/all_gather | solution.py:29
  41.8 3.9 %reshape.34 = bf16[4,2,24576]{2,1,0:T(2,128)(2,1)} reshape(bf16[6144,2,16]{2,1,0:T(2,128)(2,1)S(1)} %bitcast.39) | data formatting | bytes 786432
  45.7 11.3 %all-to-all-start.1 = ((bf16[4,2,24576]{2,1,0:T(2,128)(2,1)}), bf16[4,2,24576]{2,1,0:T(2,128)(2,1)}, u32[]{:S(2)}, u32[]{:S(2)}) async-start(bf16[4,2,24576]{2,1,0:T(2,128)(2,1)} %reshape.34), calls=%async_computation.1 | async-start | bytes 786432 | tf_op jit(solution)/shard_map/all_to_all | solution.py:33
  57.0 1.6 gather_fusion
  58.6 0.8 compare_select_fusion.1
  59.3 0.1 fusion.14
  59.4 27.0 %all_gather.6 = bf16[2,16,6144]{2,1,0:T(8,128)(2,1)} all-gather(bf16[2,16,768]{2,1,0:T(8,128)(2,1)S(1)} %fusion.14), channel_id=1, replica_groups=mesh['dp'=4,'shard'=8] {'shard'}, dimensions={2}, use_global_device_ids=true | all-gather | bytes 442368 | tf_op jit(solution)/shard_map/all_gather | solution.py:30
  86.4 6.1 %copy.24 = bf16[2,16,6144]{1,0,2:T(2,128)(2,1)S(1)} copy(bf16[2,16,6144]{2,1,0:T(8,128)(2,1)} %all_gather.6) | data formatting | bytes 786432 | tf_op jit(solution)/shard_map/all_gather | solution.py:30
  92.5 3.9 %reshape.36 = bf16[4,2,24576]{2,1,0:T(2,128)(2,1)} reshape(bf16[6144,2,16]{2,1,0:T(2,128)(2,1)S(1)} %bitcast.40) | data formatting | bytes 786432
  96.4 0.0 all-to-all-done.1
  96.4 10.1 %all-to-all-start = ((bf16[4,2,24576]{2,1,0:T(2,128)(2,1)}), bf16[4,2,24576]{2,1,0:T(2,128)(2,1)}, u32[]{:S(2)}, u32[]{:S(2)}) async-start(bf16[4,2,24576]{2,1,0:T(2,128)(2,1)} %reshape.36), calls=%async_computation | async-start | bytes 786432 | tf_op jit(solution)/shard_map/all_to_all | solution.py:34
  106.5 0.0 all-reduce.3.cloned.1.call-start
  106.5 3.5 %reshape.35 = bf16[6144,2,16]{2,1,0:T(2,128)(2,1)S(1)} reshape(bf16[4,2,24576]{2,1,0:T(2,128)(2,1)} %all-to-all-done.1) | data formatting | bytes 786432
  110.0 4.8 %copy.33 = bf16[2,16,4,1536]{3,2,1,0:T(4,128)(2,1)} copy(bf16[2,16,4,1536]{1,0,3,2:T(2,128)(2,1)S(1)} %bitcast.41) | data formatting | bytes 786432 | tf_op jit(solution)/shard_map/all_to_all | solution.py:33
  114.8 1.1 copy.29
  115.9 7.7 %convolution_convert_fusion = bf16[2,64,2048]{2,1,0:T(8,128)(2,1)} fusion(bf16[2,64,1536]{2,1,0:T(8,128)(2,1)S(1)} %bitcast.35, bf16[2,1536,2048]{2,1,0:T(8,128)(2,1)} %param.10), kind=kOutput, calls=%fused_computation.6 | convolution fusion | flops 805568512 | bytes 13500416 | tf_op jit(solution)/shard_map/erd,edf->erf/dot_general | solution.py:37
  123.6 7.7 %convolution_convert_fusion.1 = bf16[2,64,2048]{2,1,0:T(8,128)(2,1)} fusion(bf16[2,64,1536]{2,1,0:T(8,128)(2,1)S(1)} %bitcast.36, bf16[2,1536,2048]{2,1,0:T(8,128)(2,1)} %param.11), kind=kOutput, calls=%fused_computation.7 | convolution fusion | flops 805568512 | bytes 13500416 | tf_op jit(solution)/shard_map/erd,edf->erf/dot_general | solution.py:40
  131.2 0.0 copy-start.3
  131.2 0.0 all-to-all-done
  131.2 4.7 %reshape.37 = bf16[6144,2,16]{2,1,0:T(2,128)(2,1)} reshape(bf16[4,2,24576]{2,1,0:T(2,128)(2,1)} %all-to-all-done) | data formatting | bytes 786432
  135.9 7.3 %copy.32 = bf16[2,16,4,1536]{3,2,1,0:T(4,128)(2,1)S(1)} copy(bf16[2,16,4,1536]{1,0,3,2:T(2,128)(2,1)} %bitcast.42) | data formatting | bytes 786432 | tf_op jit(solution)/shard_map/all_to_all | solution.py:34
  143.2 0.1 copy.26
  143.3 9.2 %convolution_convert_fusion.2 = bf16[2,64,2048]{2,1,0:T(8,128)(2,1)} fusion(bf16[2,64,1536]{2,1,0:T(8,128)(2,1)S(1)} %bitcast.43, bf16[2,2048,1536]{2,1,0:T(8,128)(2,1)} %param.12), kind=kOutput, calls=%fused_computation.8 | convolution fusion | flops 805568512 | bytes 13500416 | tf_op jit(solution)/shard_map/erd,efd->erf/dot_general | solution.py:41
  152.5 0.0 all-reduce.3.cloned.1.call-update
  152.5 0.0 copy-done.3
  152.6 3.2 %psum.31 = s32[2,1]{0,1:T(1,128)S(1)} all-reduce(s32[2,1]{0,1:T(1,128)S(1)} %copy-done.3), channel_id=1, replica_groups=mesh['dp'=4,'shard'=8] {'dp'}, use_global_device_ids=true, to_apply=%region_4.5 | all-reduce | flops 2 | bytes 16 | tf_op jit(solution)/shard_map/psum | solution.py:36
  155.7 39.9 %all-reduce.3.cloned.1.call-done = (bf16[2,64,2048]{2,1,0:T(8,128)(2,1)}, bf16[2,64,2048]{2,1,0:T(8,128)(2,1)}, bf16[2,64,2048]{2,1,0:T(8,128)(2,1)}) async-done(((bf16[2,64,2048]{2,1,0:T(8,128)(2,1)}, bf16[2,64,2048]{2,1,0:T(8,128)(2,1)}, bf16[2,64,2048]{2,1,0:T(8,128)(2,1)}), (bf16[2,64,2048]{2,1,0:T(8,128)(2,1)}, bf16[2,64,2048]{2,1,0:T(8,128)(2,1)}, ...) | async-done | bytes 1572880 | tf_op jit(solution)/shard_map/psum | solution.py:44
  195.6 0.0 copy-start.4
  195.6 0.0 copy-start.5
  195.6 9.1 %fusion.20 = f32[2,64,1536]{2,1,0:T(8,128)S(1)} fusion(bf16[2,1536,2048]{2,1,0:T(8,128)(2,1)} %param.10, bf16[2,64,2048]{2,1,0:T(8,128)(2,1)} %get-tuple-element.4, bf16[2,64,2048]{2,1,0:T(8,128)(2,1)} %get-tuple-element.5, bf16[2,64,2048]{2,1,0:T(8,128)(2,1)} %get-tuple-element.6), kind=kOutput, calls=%fused_computation.38 | convolution fusion | flops 808714240 | bytes 14942208 | tf_op jit(solution)/shard_map/erf,edf->erd/dot_general | solution.py:63
  204.6 0.0 copy-done.4
  204.7 0.0 copy-done.5
  204.7 0.0 copy-start.6
  204.7 8.6 %fusion = bf16[2,64,1536]{2,1,0:T(8,128)(2,1)S(1)} fusion(f32[2,64,1536]{2,1,0:T(8,128)S(1)} %fusion.20, bf16[2,1536,2048]{2,1,0:T(8,128)(2,1)} %param.11, bf16[2,64,2048]{2,1,0:T(8,128)(2,1)S(1)} %copy-done.5, bf16[2,64,2048]{2,1,0:T(8,128)(2,1)S(1)} %copy-done.4), kind=kOutput, calls=%fused_computation.9 | convolution fusion | flops 807796736 | bytes 14811136 | tf_op jit(solution)/shard_map/erf,edf->erd/dot_general | solution.py:64
  213.2 1.2 copy.30
  214.4 5.2 %all-to-all-start.2 = ((bf16[2,64,1536]{2,0,1:T(2,128)(2,1)}), bf16[2,64,1536]{2,0,1:T(2,128)(2,1)S(1)}, u32[]{:S(2)}, u32[]{:S(2)}) async-start(bf16[2,64,1536]{2,0,1:T(2,128)(2,1)} %copy.30), calls=%async_computation.2 | async-start | bytes 786432 | tf_op jit(solution)/shard_map/all_to_all | solution.py:66
  219.6 0.0 reduce-scatter.2.cloned.1.call-start
  219.6 0.0 copy-done.6
  219.6 6.7 %divide_convert_fusion.2 = bf16[2,1536,2048]{2,1,0:T(8,128)(2,1)} fusion(f32[2]{0:T(128)S(1)} %convert_bitcast_fusion, bf16[2,64,1536]{2,1,0:T(8,128)(2,1)S(1)} %bitcast.37, bf16[2,64,2048]{2,1,0:T(8,128)(2,1)S(1)} %copy-done.6, bf16[2,64,2048]{2,1,0:T(8,128)(2,1)S(1)} %copy-done.4, bf16[2,64,2048]{2,1,0:T(8,128)(2,1)S(1)} %copy-done.5), kind=kOutput, calls=%fused_computation.4 | convolution fusion | flops 821297152 | bytes 14549000 | tf_op jit(solution)/shard_map/erd,erf->edf/dot_general | solution.py:55
  226.3 6.9 %divide_convert_fusion = bf16[2,2048,1536]{2,1,0:T(8,128)(2,1)} fusion(f32[2]{0:T(128)S(1)} %convert_bitcast_fusion, bf16[2,64,1536]{2,1,0:T(8,128)(2,1)S(1)} %bitcast.44, bf16[2,64,2048]{2,1,0:T(8,128)(2,1)S(1)} %copy-done.6, bf16[2,64,2048]{2,1,0:T(8,128)(2,1)S(1)} %copy-done.5), kind=kOutput, calls=%fused_computation.2 | convolution fusion | flops 819986432 | bytes 14024712 | tf_op jit(solution)/shard_map/erf,erd->efd/dot_general | solution.py:51
  233.2 0.0 all-to-all-done.2
  233.2 0.3 copy.31
  233.5 1.0 all_to_all.50
  234.5 0.0 reduce-scatter.2.cloned.1.call-update
  234.6 0.0 copy-start.2
  234.6 0.0 copy-start.1
  234.6 6.7 %divide_convert_fusion.1 = bf16[2,1536,2048]{2,1,0:T(8,128)(2,1)} fusion(f32[2]{0:T(128)S(1)} %convert_bitcast_fusion, bf16[2,64,1536]{2,1,0:T(8,128)(2,1)S(1)} %bitcast.38, bf16[2,64,2048]{2,1,0:T(8,128)(2,1)S(1)} %copy-done.5, bf16[2,64,2048]{2,1,0:T(8,128)(2,1)S(1)} %copy-done.4), kind=kOutput, calls=%fused_computation.3 | convolution fusion | flops 819986432 | bytes 14024712 | tf_op jit(solution)/shard_map/erd,erf->edf/dot_general | solution.py:59
  241.3 54.3 %reduce-scatter.2.cloned.1.call-done = bf16[2,16,768]{2,1,0:T(8,128)(2,1)} async-done(((bf16[2,16,6144]{2,1,0:T(8,128)(2,1)}), bf16[2,16,768]{2,1,0:T(8,128)(2,1)}) %reduce-scatter.2.cloned.1.call-update) | async-done | bytes 49168 | tf_op jit(solution)/shard_map/reduce_scatter | solution.py:67
  295.7 0.0 copy-done.2
  295.7 1.7 fusion.1
  297.4 0.0 copy-done.1
  (2 shorter events, 0.0 us)
Async XLA Ops:
  7.2 0.9 copy-start
  45.7 50.6 %all-to-all-start.1 = ((bf16[4,2,24576]{2,1,0:T(2,128)(2,1)}), bf16[4,2,24576]{2,1,0:T(2,128)(2,1)}, u32[]{:S(2)}, u32[]{:S(2)}) async-start(bf16[4,2,24576]{2,1,0:T(2,128)(2,1)} %reshape.34), calls=%async_computation.1 | async-start | bytes 786432 | tf_op jit(solution)/shard_map/all_to_all | solution.py:33
  96.4 34.8 %all-to-all-start = ((bf16[4,2,24576]{2,1,0:T(2,128)(2,1)}), bf16[4,2,24576]{2,1,0:T(2,128)(2,1)}, u32[]{:S(2)}, u32[]{:S(2)}) async-start(bf16[4,2,24576]{2,1,0:T(2,128)(2,1)} %reshape.36), calls=%async_computation | async-start | bytes 786432 | tf_op jit(solution)/shard_map/all_to_all | solution.py:34
  106.5 89.1 %all-reduce.3.cloned.1.call-start = ((), (), s32[]{:S(2)}) async-start(), calls=%async_computation.5 | async-start | bytes 3145728 | tf_op jit(solution)/shard_map/psum | solution.py:44
  131.2 21.3 %copy-start.3 = (s32[2,1]{0,1:T(1,128)S(1)}, s32[2,1]{0,1:T(1,128)}, u32[]{:S(2)}) copy-start(s32[2,1]{0,1:T(1,128)} %param.15) | copy-start | bytes 28
  195.6 9.1 %copy-start.4 = (bf16[2,64,2048]{2,1,0:T(8,128)(2,1)S(1)}, bf16[2,64,2048]{2,1,0:T(8,128)(2,1)}, u32[]{:S(2)}) copy-start(bf16[2,64,2048]{2,1,0:T(8,128)(2,1)} %get-tuple-element.5) | copy-start | bytes 1572868
  195.6 9.1 %copy-start.5 = (bf16[2,64,2048]{2,1,0:T(8,128)(2,1)S(1)}, bf16[2,64,2048]{2,1,0:T(8,128)(2,1)}, u32[]{:S(2)}) copy-start(bf16[2,64,2048]{2,1,0:T(8,128)(2,1)} %get-tuple-element.6) | copy-start | bytes 1572868
  204.7 14.9 %copy-start.6 = (bf16[2,64,2048]{2,1,0:T(8,128)(2,1)S(1)}, bf16[2,64,2048]{2,1,0:T(8,128)(2,1)}, u32[]{:S(2)}) copy-start(bf16[2,64,2048]{2,1,0:T(8,128)(2,1)} %get-tuple-element.4) | copy-start | bytes 1572868
  214.4 18.8 %all-to-all-start.2 = ((bf16[2,64,1536]{2,0,1:T(2,128)(2,1)}), bf16[2,64,1536]{2,0,1:T(2,128)(2,1)S(1)}, u32[]{:S(2)}, u32[]{:S(2)}) async-start(bf16[2,64,1536]{2,0,1:T(2,128)(2,1)} %copy.30), calls=%async_computation.2 | async-start | bytes 786432 | tf_op jit(solution)/shard_map/all_to_all | solution.py:66
  219.6 76.1 %reduce-scatter.2.cloned.1.call-start = ((), (), s32[]{:S(2)}) async-start(), calls=%async_computation.4 | async-start | bytes 442368 | tf_op jit(solution)/shard_map/reduce_scatter | solution.py:67
  234.6 61.1 %copy-start.2 = (s32[2,16]{1,0:T(2,128)S(1)}, s32[2,16]{1,0:T(2,128)}, u32[]{:S(2)}) copy-start(s32[2,16]{1,0:T(2,128)} %param.13) | copy-start | bytes 388
  234.6 62.8 %copy-start.1 = (bf16[64,768]{1,0:T(8,128)(2,1)S(1)}, bf16[64,768]{1,0:T(8,128)(2,1)}, u32[]{:S(2)}) copy-start(bf16[64,768]{1,0:T(8,128)(2,1)} %param.8) | copy-start | bytes 294916
Sparse Core Ops, SparseCore 0:
  152.7 42.8 all-reduce.2
  234.7 60.9 reduce-scatter.1
where the time goes:
time: 309 us; the launch traced here: 304 us
  waiting for transfers between devices  94.3 us (31%)
  matrix products  64.3 us (21%)
  blocking collectives  57.2 us (19%)
  local copies, waits for them, and re-layouts  46.3 us (15%)
  starting transfers between devices  26.5 us (9%)
  between operations  14.2 us (5%)
    reduce_scatter x1, waiting for transfers between devices, on_device(): lax.psum_scatter(owned_rows.astype(jnp.float32).astype(jnp.bfloat16), 'sh...  54.3 us
    psum x1, waiting for transfers between devices, on_device(): lax.psum(up_part.astype(jnp.bfloat16), 'dp').astype(jnp.float32)  39.9 us
    all_gather x1, blocking collectives, on_device(): lax.all_gather(picked, 'shard', axis=2, tiled=True)  27 us
    all_gather x1, blocking collectives, on_device(): lax.all_gather(weighted, 'shard', axis=2, tiled=True)  27 us
    unnamed x18, local copies, waits for them, and re-layouts  16.1 us
    all_to_all x1, starting transfers between devices, on_device(): lax.all_to_all(full_rows, 'dp', split_axis=2, concat_axis=1, tiled=True)  11.3 us
    all_to_all x1, starting transfers between devices, on_device(): lax.all_to_all(full_cot, 'dp', split_axis=2, concat_axis=1, tiled=True)  10.1 us
    dot_general x1, matrix products, on_device(): jnp.einsum('erd,efd->erf', block_cot, down_proj, preferred_element_type=j...  9.24 us
  transfers between devices with their start and end apart: 5, of which 2 were waited for; matrix products, arithmetic and copies ran while one was open for 19% of the time, Pallas kernels for 0%

commit v1 on v0

--- a/solution.py
+++ b/solution.py
@@ -1,7 +1,14 @@
+import functools
+
 import jax
 import jax.numpy as jnp
 from jax import lax
+from jax.experimental import pallas as pl
+from jax.experimental.pallas import tpu as pltpu
 from jax.sharding import PartitionSpec as P
+
+MESH = pl.DeviceIdType.MESH
+PIECES = 2
 
 
 def slope_terms(gate_sum, up_sum, cot_hidden):
@@ -78,6 +85,330 @@
     return (grad_tokens, grad_gate_proj, grad_up_proj, grad_down_proj)
 
 
+def step_kernel(
+    n_dp, n_shard,
+    slot_col, slot_row, scale_col, counts, tokens, cot, gate_hbm, up_hbm, down_hbm,
+    rows_out, cotr_out, hid_out, gg_out, gu_out, tot_out, tok_out,
+    gate_w, up_w, down_w, pick, wcot, mine, psend, precv, xsend, xrecv, back, parts, cnt_in,
+    w_sem, g_send, g_recv, p_send, p_recv, x_send, x_recv, a_send, a_recv, r_send, r_recv,
+):
+    d = lax.axis_index("dp")
+    s = lax.axis_index("shard")
+    experts, depth, width = gate_w.shape
+    feats = tokens.shape[1]
+    slots = slot_col.shape[0] // experts
+    per = n_shard // n_dp
+    core = d % 2
+    pair = d + 1 - 2 * core
+    across = (d + 2) % 4
+    half = width // 2
+    piece = half // PIECES
+
+    loads = []
+    for e in range(experts):
+        for i, (src, dst) in enumerate(((gate_hbm, gate_w), (up_hbm, up_w), (down_hbm, down_w))):
+            load = pltpu.make_async_copy(src.at[e], dst.at[e], w_sem.at[i, e])
+            load.start()
+            loads.append(load)
+
+    barrier = pltpu.get_barrier_semaphore()
+    owner = s // per
+    for t in range(n_shard):
+        pl.semaphore_signal(barrier, inc=1, device_id={"dp": owner, "shard": t}, device_id_type=MESH)
+    for e in range(n_dp):
+        for k in range(per):
+            pl.semaphore_signal(
+                barrier, inc=1, device_id={"dp": e, "shard": d * per + k}, device_id_type=MESH
+            )
+    for peer in (pair, across):
+        pl.semaphore_signal(barrier, inc=1, device_id={"dp": peer, "shard": s}, device_id_type=MESH)
+
+    token_ids = lax.broadcasted_iota(jnp.int32, (experts * slots, tokens.shape[0]), 1)
+    choose = (slot_col[...] == token_ids).astype(jnp.float32).astype(jnp.bfloat16)
+    pick_all = jnp.dot(choose, tokens[...], preferred_element_type=jnp.float32)
+    cot_all = jnp.dot(choose, cot[...], preferred_element_type=jnp.float32)
+    cot_all = (cot_all * scale_col[...]).astype(jnp.bfloat16)
+    pick_all = pick_all.astype(jnp.bfloat16)
+    for e in range(experts):
+        pick[e] = pick_all[e * slots : (e + 1) * slots]
+        wcot[e] = cot_all[e * slots : (e + 1) * slots]
+
+    pl.semaphore_wait(barrier, n_shard + n_dp * per + 2)
+
+    k_me = s % per
+    at_me = d * per + k_me
+    row_me = pl.ds(pl.multiple_of(d * slots, slots), slots)
+    col_me = pl.ds(pl.multiple_of(k_me * feats, 128), feats)
+    sends = []
+
+    def send_to(target, is_self, pairs, send_sem_of, recv_sem_of):
+        for i, (src, dst) in enumerate(pairs):
+            remote = pltpu.make_async_remote_copy(
+                src_ref=src, dst_ref=dst, send_sem=send_sem_of(i), recv_sem=recv_sem_of(i),
+                device_id=target, device_id_type=MESH,
+            )
+
+            @pl.when(jnp.logical_not(is_self))
+            def _():
+                remote.start()
+
+            @pl.when(is_self)
+            def _():
+                pltpu.make_async_copy(src, dst, recv_sem_of(i)).start()
+
+            sends.append((remote, is_self))
+
+    gather_pairs = (
+        (pick, rows_out.at[:, row_me, col_me]),
+        (wcot, cotr_out.at[:, row_me, col_me]),
+        (counts, cnt_in.at[at_me]),
+    )
+    for step in range(n_shard):
+        t = (s + step) % n_shard
+        send_to(
+            {"dp": owner, "shard": t},
+            jnp.logical_and(owner == d, t == s),
+            gather_pairs,
+            lambda i: g_send.at[i, step],
+            lambda i: g_recv.at[i, at_me],
+        )
+    for e in range(n_dp):
+        for k in range(per):
+            at = e * per + k
+            r = pl.ds(e * slots, slots)
+            c = pl.ds(k * feats, feats)
+            for i, dst in enumerate(
+                (rows_out.at[:, r, c], cotr_out.at[:, r, c], cnt_in.at[at])
+            ):
+                pltpu.make_async_copy(dst, dst, g_recv.at[i, at]).wait()
+    total = cnt_in[0]
+    for e in range(1, n_dp):
+        total = total + cnt_in[e * per]
+    tot_out[...] = total
+
+    stages = [(e, j) for e in range(experts) for j in range(PIECES)]
+
+    def columns(who, j):
+        return pl.ds(pl.multiple_of(who * half + j * piece, 128), piece)
+
+    def partials(e, cols):
+        rows = rows_out[e]
+        gate = jnp.dot(rows, gate_w[e, :, cols], preferred_element_type=jnp.float32)
+        up = jnp.dot(rows, up_w[e, :, cols], preferred_element_type=jnp.float32)
+        down = lax.dot_general(
+            cotr_out[e], down_w[e, cols, :], (((1,), (1,)), ((), ())),
+            preferred_element_type=jnp.float32,
+        )
+        return gate, up, down
+
+    def pair_copy(t):
+        return pltpu.make_async_remote_copy(
+            src_ref=psend.at[t], dst_ref=precv.at[t], send_sem=p_send.at[t], recv_sem=p_recv.at[t],
+            device_id={"dp": pair, "shard": s}, device_id_type=MESH,
+        )
+
+    def across_copy(t):
+        return pltpu.make_async_remote_copy(
+            src_ref=xsend.at[t], dst_ref=xrecv.at[t], send_sem=x_send.at[t], recv_sem=x_recv.at[t],
+            device_id={"dp": across, "shard": s}, device_id_type=MESH,
+        )
+
+    def back_copies(t, who):
+        e, j = stages[t]
+        cols = columns(who, j)
+        return [
+            pltpu.make_async_remote_copy(
+                src_ref=out.at[e, :, cols], dst_ref=out.at[e, :, cols],
+                send_sem=a_send.at[i, t], recv_sem=a_recv.at[i, t],
+                device_id={"dp": pair, "shard": s}, device_id_type=MESH,
+            )
+            for i, out in enumerate((hid_out, gg_out, gu_out))
+        ]
+
+    def compute(t):
+        e, j = stages[t]
+        if j == 0:
+            for load in loads[3 * e : 3 * e + 3]:
+                load.wait()
+        for i, value in enumerate(partials(e, columns(1 - core, j))):
+            psend[t, i] = value.astype(jnp.bfloat16)
+        pair_copy(t).start()
+        for i, value in enumerate(partials(e, columns(core, j))):
+            mine[t, i] = value.astype(jnp.bfloat16)
+
+    def add_pair(t):
+        pair_copy(t).wait_recv()
+        both = mine[t].astype(jnp.float32) + precv[t].astype(jnp.float32)
+        xsend[t] = both.astype(jnp.bfloat16)
+        across_copy(t).start()
+
+    def finish(t):
+        e, j = stages[t]
+        across_copy(t).wait_recv()
+        gate = xsend[t, 0].astype(jnp.float32) + xrecv[t, 0].astype(jnp.float32)
+        up = xsend[t, 1].astype(jnp.float32) + xrecv[t, 1].astype(jnp.float32)
+        cot_hidden = xsend[t, 2].astype(jnp.float32) + xrecv[t, 2].astype(jnp.float32)
+        cols = columns(core, j)
+        hid_out[e, :, cols] = (jax.nn.silu(gate) * up).astype(jnp.bfloat16)
+        grad_gate, grad_up = slope_terms(gate, up, cot_hidden)
+        gg_out[e, :, cols] = grad_gate
+        gu_out[e, :, cols] = grad_up
+        for copy in back_copies(t, core):
+            copy.start()
+
+    def backward(e):
+        for t, (te, _) in enumerate(stages):
+            if te == e:
+                for copy in back_copies(t, 1 - core):
+                    copy.wait_recv()
+        contract = (((1,), (1,)), ((), ()))
+        block = 256 if depth % 256 == 0 else depth
+        for b in range(depth // block):
+            r = pl.ds(b * block, block)
+            term = lax.dot_general(
+                gg_out[e], gate_w[e, r, :], contract, preferred_element_type=jnp.float32
+            ) + lax.dot_general(
+                gu_out[e], up_w[e, r, :], contract, preferred_element_type=jnp.float32
+            )
+            back[e, :, r] = term.astype(jnp.bfloat16)
+        for step in range(n_dp):
+            who = (d + step) % n_dp
+            r = pl.ds(pl.multiple_of(who * slots, slots), slots)
+            for k in range(per):
+                send_to(
+                    {"dp": who, "shard": d * per + k},
+                    jnp.logical_and(who == d, d * per + k == s),
+                    ((back.at[e, r, pl.ds(k * feats, feats)], parts.at[e, s]),),
+                    lambda i: r_send.at[e, step * per + k],
+                    lambda i: r_recv.at[e, s],
+                )
+
+    last = len(stages)
+    for t in range(last):
+        compute(t)
+        if t >= 1:
+            add_pair(t - 1)
+        if t >= 2:
+            finish(t - 2)
+    add_pair(last - 1)
+    finish(last - 2)
+    for e in range(experts - 1):
+        backward(e)
+    finish(last - 1)
+    backward(experts - 1)
+
+    choose_back = (
+        slot_row[...] == lax.broadcasted_iota(jnp.int32, (tokens.shape[0], experts * slots), 0)
+    ).astype(jnp.float32)
+    sums = []
+    for e in range(experts):
+        for t in range(n_shard):
+            pltpu.make_async_copy(parts.at[e, t], parts.at[e, t], r_recv.at[e, t]).wait()
+        acc = parts[e, 0].astype(jnp.float32)
+        for t in range(1, n_shard):
+            acc = acc + parts[e, t].astype(jnp.float32)
+        sums.append(acc)
+    tok_out[...] = jnp.dot(
+        choose_back, jnp.concatenate(sums, axis=0),
+        preferred_element_type=jnp.float32, precision=lax.Precision.HIGHEST,
+    ).astype(jnp.bfloat16)
+
+    for t in range(last):
+        pair_copy(t).wait_send()
+        across_copy(t).wait_send()
+        for copy in back_copies(t, core):
+            copy.wait_send()
+    for remote, is_self in sends:
+
+        @pl.when(jnp.logical_not(is_self))
+        def _():
+            remote.wait_send()
+
+
+def on_device_fused(
+    n_dp, n_shard,
+    tokens, cotangent, gate_proj, up_proj, down_proj, slot_tokens, gate_weights, live_counts,
+):
+    experts, slots = slot_tokens.shape
+    depth, width = gate_proj.shape[1:]
+    feats = tokens.shape[1]
+    routed = slots * n_dp
+    per = n_shard // n_dp
+    position = lax.broadcasted_iota(jnp.int32, slot_tokens.shape, 1)
+    alive_mask = (position < live_counts).astype(jnp.float32)
+    scale_col = (gate_weights * alive_mask).reshape(-1, 1)
+    counts = jnp.broadcast_to(
+        jnp.pad(live_counts, ((0, 8 - experts), (0, 0))), (8, 128)
+    ).astype(jnp.int32)
+    stages = experts * PIECES
+    piece = width // 2 // PIECES
+    vmem = pl.BlockSpec(memory_space=pltpu.VMEM)
+    hbm = pl.BlockSpec(memory_space=pl.ANY)
+    bf16 = jnp.bfloat16
+    dma = pltpu.SemaphoreType.DMA
+    block = pltpu.VMEM((stages, 3, routed, piece), bf16)
+    outs = pl.pallas_call(
+        functools.partial(step_kernel, n_dp, n_shard),
+        out_shape=(
+            jax.ShapeDtypeStruct((experts, routed, depth), bf16),
+            jax.ShapeDtypeStruct((experts, routed, depth), bf16),
+            jax.ShapeDtypeStruct((experts, routed, width), bf16),
+            jax.ShapeDtypeStruct((experts, routed, width), bf16),
+            jax.ShapeDtypeStruct((experts, routed, width), bf16),
+            jax.ShapeDtypeStruct((8, 128), jnp.int32),
+            jax.ShapeDtypeStruct(tokens.shape, bf16),
+        ),
+        in_specs=[vmem] * 6 + [hbm] * 3,
+        out_specs=(vmem,) * 7,
+        scratch_shapes=[
+            pltpu.VMEM((experts, depth, width), bf16),
+            pltpu.VMEM((experts, depth, width), bf16),
+            pltpu.VMEM((experts, width, depth), bf16),
+            pltpu.VMEM((experts, slots, feats), bf16),
+            pltpu.VMEM((experts, slots, feats), bf16),
+            block, block, block, block, block,
+            pltpu.VMEM((experts, routed, depth), bf16),
+            pltpu.VMEM((experts, n_shard, slots, feats), bf16),
+            pltpu.VMEM((n_dp * per, 8, 128), jnp.int32),
+            dma((3, experts)),
+            dma((3, n_shard)), dma((3, n_dp * per)),
+            dma((stages,)), dma((stages,)), dma((stages,)), dma((stages,)),
+            dma((3, stages)), dma((3, stages)),
+            dma((experts, n_dp * per)), dma((experts, n_shard)),
+        ],
+        compiler_params=pltpu.CompilerParams(
+            collective_id=0, has_side_effects=True, vmem_limit_bytes=62 * 1024 * 1024
+        ),
+        name="route_step",
+    )(
+        slot_tokens.reshape(-1, 1), slot_tokens.reshape(1, -1), scale_col, counts,
+        tokens, cotangent, gate_proj, up_proj, down_proj,
+    )
+    block_rows, block_cot, hidden_all, gate_all, up_all, totals, grad_tokens = outs
+    scale_back = totals[:experts, :1].astype(jnp.float32)[:, :, None]
+    grad_down_proj = (
+        jnp.einsum("erf,erd->efd", hidden_all, block_cot, preferred_element_type=jnp.float32)
+        / scale_back
+    ).astype(jnp.bfloat16)
+    grad_gate_proj = (
+        jnp.einsum("erd,erf->edf", block_rows, gate_all, preferred_element_type=jnp.float32)
+        / scale_back
+    ).astype(jnp.bfloat16)
+    grad_up_proj = (
+        jnp.einsum("erd,erf->edf", block_rows, up_all, preferred_element_type=jnp.float32)
+        / scale_back
+    ).astype(jnp.bfloat16)
+    return (grad_tokens, grad_gate_proj, grad_up_proj, grad_down_proj)
+
+
+def pick_form(n_dp, n_shard, *args):
+    feats = args[0].shape[1]
+    aligned = feats % 128 == 0 and args[2].shape[2] % (256 * PIECES) == 0
+    if n_dp == 4 and n_shard % n_dp == 0 and aligned and args[5].shape[1] % 16 == 0:
+        return on_device_fused(n_dp, n_shard, *args)
+    return on_device(*args)
+
+
 def solution(mesh):
     in_specs = (
         P("dp", "shard"),
@@ -96,5 +427,5 @@
         P(None, "shard", "dp"),
     )
     return jax.shard_map(
-        on_device, mesh=mesh, in_specs=in_specs, out_specs=out_specs, check_vma=False
-    )
+        functools.partial(pick_form, mesh.shape["dp"], mesh.shape["shard"]), mesh=mesh, in_specs=in_specs, out_specs=out_specs, check_vma=False
+    )

time: 309 us -> 99 us (0.32); the launches traced: 304 us -> 98.7 us
  waiting for transfers between devices: 94.3 us -> 0 us
  Pallas kernels: 0 us -> 68 us
  blocking collectives: 57.2 us -> 0 us
  matrix products: 64.3 us -> 23.2 us
  local copies, waits for them, and re-layouts: 46.3 us -> 5.31 us
  starting transfers between devices: 26.5 us -> 0 us
  between operations: 14.2 us -> 0.66 us
    pallas_call x0 -> x1, Pallas kernels: none -> 68 us  [on_device_fused(): pl.pallas_call(functools.partial(step_kernel, n_dp, n_shard), out_shape=(...]
    reduce_scatter x1 -> x0, waiting for transfers between devices: 54.3 us -> none  [on_device(): lax.psum_scatter(owned_rows.astype(jnp.float32).astype(jnp.bfloat16), 'sh...]
    all_gather x2 -> x0, blocking collectives: 54 us -> none  [the longest x1 27 us: on_device(): lax.all_gather(picked, 'shard', axis=2, tiled=True)]
    dot_general x9 -> x3, matrix products: 64.3 us -> 23.2 us  [the longest x1 9.78 us: on_device_fused(): jnp.einsum('erf,erd->efd', hidden_all, block_cot, preferred_element_type=...]
    psum x1 -> x0, waiting for transfers between devices: 39.9 us -> none  [on_device(): lax.psum(up_part.astype(jnp.bfloat16), 'dp').astype(jnp.float32)]
    all_to_all x3 -> x0, starting transfers between devices: 26.5 us -> none  [the longest x1 11.3 us: on_device(): lax.all_to_all(full_rows, 'dp', split_axis=2, concat_axis=1, tiled=True)]
    unnamed x18 -> x9, local copies, waits for them, and re-layouts: 16.1 us -> 0.66 us
    all_to_all x6 -> x0, local copies, waits for them, and re-layouts: 14.6 us -> none  [the longest x2 7.36 us: on_device(): lax.all_to_all(full_cot, 'dp', split_axis=2, concat_axis=1, tiled=True)]
  transfers between devices with their start and end apart: 5 -> 0, of which waited for: 2 -> 0; matrix products, arithmetic and copies ran while one was open for 19% -> 0% of each run, Pallas kernels for 0% -> 0%
where the time goes in v1:
time: 99 us; the launch traced here: 98.7 us
  Pallas kernels  68 us (69%)
  matrix products  23.2 us (23%)
  local copies, waits for them, and re-layouts  5.31 us (5%)
  other arithmetic  1.55 us (2%)
    pallas_call x1, Pallas kernels, on_device_fused(): pl.pallas_call(functools.partial(step_kernel, n_dp, n_shard), out_shape=(...  68 us
    dot_general x1, matrix products, on_device_fused(): jnp.einsum('erf,erd->efd', hidden_all, block_cot, preferred_element_type=...  9.78 us
    dot_general x1, matrix products, on_device_fused(): jnp.einsum('erd,erf->edf', block_rows, up_all, preferred_element_type=jnp...  6.74 us
    dot_general x1, matrix products, on_device_fused(): jnp.einsum('erd,erf->edf', block_rows, gate_all, preferred_element_type=j...  6.72 us

profile of v1, /device:TPU:3, one launch (start us, length us, event | category | flops | bytes accessed | tf_op | source)
XLA Modules:
  0.0 98.7 jit_solution(9093303161281102467)
XLA Ops:
  0.6 1.3 %reshape.19.slot_row = s32[1,32]{1,0:T(1,128)} reshape(s32[2,16]{1,0:T(2,128)} %param.13) | data formatting | bytes 256 | tf_op jit(solution)/shard_map/reshape | solution.py:384
  1.9 0.7 pad_bitcast_fusion
  2.6 0.8 compare_select_fusion
  3.3 0.7 broadcast_in_dim.9.counts
  4.0 0.7 reshape.22.scale_col
  4.7 1.4 %reshape.21.slot_col = s32[32,1]{1,0:T(8,128)} reshape(s32[2,16]{1,0:T(2,128)} %param.13) | data formatting | bytes 256 | tf_op jit(solution)/shard_map/reshape | solution.py:384
  6.0 68.0 %route_step.1 = (bf16[2,64,1536]{2,1,0:T(8,128)(2,1)}, bf16[2,64,1536]{2,1,0:T(8,128)(2,1)}, bf16[2,64,2048]{2,1,0:T(8,128)(2,1)}, bf16[2,64,2048]{2,1,0:T(8,128...) custom-call(s32[32,1]{1,0:T(8,128)} %reshape.21.slot_col, ...), custom_call_target="tpu_custom_call" | custom-call | tf_op jit(solution)/shard_map/route_step/pallas_call | solution.py:350
  74.0 0.8 convert_reduce_fusion
  74.8 0.0 copy-start.2
  74.8 0.0 copy-start.3
  74.8 9.8 %divide_convert_fusion = bf16[2,2048,1536]{2,1,0:T(8,128)(2,1)} fusion(f32[2]{0:T(128)S(1)} %convert_reduce_fusion, bf16[2,64,2048]{2,1,0:T(8,128)(2,1)} %get-tuple-element.16, bf16[2,64,1536]{2,1,0:T(8,128)(2,1)} %get-tuple-element.17), kind=kOutput, calls=%fused_computation | convolution fusion | flops 817889280 | bytes 13500424 | tf_op jit(solution)/shard_map/erf,erd->efd/dot_general | solution.py:390
  84.6 0.0 copy-done.2
  84.6 0.0 copy-done.3
  84.6 0.0 copy-start.1
  84.6 6.7 %divide_convert_fusion.1 = bf16[2,1536,2048]{2,1,0:T(8,128)(2,1)} fusion(f32[2]{0:T(128)S(1)} %convert_reduce_fusion, bf16[2,64,1536]{2,1,0:T(8,128)(2,1)S(1)} %copy-done.3, bf16[2,64,2048]{2,1,0:T(8,128)(2,1)S(1)} %copy-done.2), kind=kOutput, calls=%fused_computation.1 | convolution fusion | flops 817889280 | bytes 13500424 | tf_op jit(solution)/shard_map/erd,erf->edf/dot_general | solution.py:398
  91.4 0.0 copy-done.1
  91.4 0.0 copy-start
  91.4 6.7 %divide_convert_fusion.2 = bf16[2,1536,2048]{2,1,0:T(8,128)(2,1)} fusion(f32[2]{0:T(128)S(1)} %convert_reduce_fusion, bf16[2,64,1536]{2,1,0:T(8,128)(2,1)S(1)} %copy-done.3, bf16[2,64,2048]{2,1,0:T(8,128)(2,1)S(1)} %copy-done.1), kind=kOutput, calls=%fused_computation.2 | convolution fusion | flops 817889280 | bytes 13500424 | tf_op jit(solution)/shard_map/erd,erf->edf/dot_general | solution.py:394
  98.1 0.0 copy-done
  98.1 0.6 copy.17
Async XLA Ops:
  74.8 9.8 %copy-start.2 = (bf16[2,64,2048]{2,1,0:T(8,128)(2,1)S(1)}, bf16[2,64,2048]{2,1,0:T(8,128)(2,1)}, u32[]{:S(2)}) copy-start(bf16[2,64,2048]{2,1,0:T(8,128)(2,1)} %get-tuple-element.15) | copy-start | bytes 1572868
  74.8 9.8 %copy-start.3 = (bf16[2,64,1536]{2,1,0:T(8,128)(2,1)S(1)}, bf16[2,64,1536]{2,1,0:T(8,128)(2,1)}, u32[]{:S(2)}) copy-start(bf16[2,64,1536]{2,1,0:T(8,128)(2,1)} %get-tuple-element.12) | copy-start | bytes 1179652
  84.6 6.7 %copy-start.1 = (bf16[2,64,2048]{2,1,0:T(8,128)(2,1)S(1)}, bf16[2,64,2048]{2,1,0:T(8,128)(2,1)}, u32[]{:S(2)}) copy-start(bf16[2,64,2048]{2,1,0:T(8,128)(2,1)} %get-tuple-element.13) | copy-start | bytes 1572868
  91.4 6.7 %copy-start = (bf16[64,768]{1,0:T(8,128)(2,1)S(1)}, bf16[64,768]{1,0:T(8,128)(2,1)}, u32[]{:S(2)}) copy-start(bf16[64,768]{1,0:T(8,128)(2,1)} %get-tuple-element.22) | copy-start | bytes 294916

commit v2 on v1

--- a/solution.py
+++ b/solution.py
@@ -87,16 +87,16 @@
 
 def step_kernel(
     n_dp, n_shard,
-    slot_col, slot_row, scale_col, counts, tokens, cot, gate_hbm, up_hbm, down_hbm,
+    slot_ids, weights, live, tokens, cot, gate_hbm, up_hbm, down_hbm,
     rows_out, cotr_out, hid_out, gg_out, gu_out, tot_out, tok_out,
-    gate_w, up_w, down_w, pick, wcot, mine, psend, precv, xsend, xrecv, back, parts, cnt_in,
-    w_sem, g_send, g_recv, p_send, p_recv, x_send, x_recv, a_send, a_recv, r_send, r_recv,
+    gate_w, up_w, down_w, pick, full, mine, psend, precv, xsend, xrecv, back, parts, cnt, cnt_in,
+    w_sem, g_send, g_recv, c_send, c_recv, b_send, b_recv, p_send, p_recv, x_send, x_recv, a_send, a_recv, r_send, r_recv,
 ):
     d = lax.axis_index("dp")
     s = lax.axis_index("shard")
     experts, depth, width = gate_w.shape
     feats = tokens.shape[1]
-    slots = slot_col.shape[0] // experts
+    slots = slot_ids.shape[1]
     per = n_shard // n_dp
     core = d % 2
     pair = d + 1 - 2 * core
@@ -120,25 +120,44 @@
             pl.semaphore_signal(
                 barrier, inc=1, device_id={"dp": e, "shard": d * per + k}, device_id_type=MESH
             )
+    for t in range(n_shard):
+        pl.semaphore_signal(barrier, inc=1, device_id={"dp": d, "shard": t}, device_id_type=MESH)
     for peer in (pair, across):
         pl.semaphore_signal(barrier, inc=1, device_id={"dp": peer, "shard": s}, device_id_type=MESH)
 
-    token_ids = lax.broadcasted_iota(jnp.int32, (experts * slots, tokens.shape[0]), 1)
-    choose = (slot_col[...] == token_ids).astype(jnp.float32).astype(jnp.bfloat16)
-    pick_all = jnp.dot(choose, tokens[...], preferred_element_type=jnp.float32)
-    cot_all = jnp.dot(choose, cot[...], preferred_element_type=jnp.float32)
-    cot_all = (cot_all * scale_col[...]).astype(jnp.bfloat16)
-    pick_all = pick_all.astype(jnp.bfloat16)
+    count = tokens.shape[0]
+    diagonal = lax.broadcasted_iota(jnp.int32, (slots, slots), 0) == lax.broadcasted_iota(
+        jnp.int32, (slots, slots), 1
+    )
+
+    def as_column(row):
+        wide = jnp.broadcast_to(row, (slots, slots))
+        return jnp.sum(jnp.where(diagonal, wide, 0.0), axis=1, keepdims=True)
+
+    cnt[...] = jnp.zeros_like(cnt)
+    token_ids = lax.broadcasted_iota(jnp.int32, (slots, count), 1).astype(jnp.float32)
     for e in range(experts):
-        pick[e] = pick_all[e * slots : (e + 1) * slots]
-        wcot[e] = cot_all[e * slots : (e + 1) * slots]
-
-    pl.semaphore_wait(barrier, n_shard + n_dp * per + 2)
+        alive = lax.broadcasted_iota(jnp.int32, (1, slots), 1) < live[e : e + 1, :]
+        scale = as_column(weights[e : e + 1, :] * alive.astype(jnp.float32))
+        chosen = as_column(slot_ids[e : e + 1, :].astype(jnp.float32)) == token_ids
+        chosen = chosen.astype(jnp.float32).astype(jnp.bfloat16)
+        picked = jnp.dot(chosen, tokens[...], preferred_element_type=jnp.float32)
+        pick[e] = picked.astype(jnp.bfloat16)
+        cots = jnp.dot(chosen, cot[...], preferred_element_type=jnp.float32)
+        pick[experts + e] = (cots * scale).astype(jnp.bfloat16)
+        cnt[e : e + 1, :] = jnp.broadcast_to(live[e : e + 1, :], (1, cnt.shape[1]))
+
+    pl.semaphore_wait(barrier, 2 * n_shard + n_dp * per + 2)
 
     k_me = s % per
     at_me = d * per + k_me
     row_me = pl.ds(pl.multiple_of(d * slots, slots), slots)
-    col_me = pl.ds(pl.multiple_of(k_me * feats, 128), feats)
+    cuts = n_shard // (2 * experts)
+    cut = feats // cuts
+
+    def cut_cols(k, c):
+        return pl.ds(pl.multiple_of(k * feats + c * cut, 128), cut)
+
     sends = []
 
     def send_to(target, is_self, pairs, send_sem_of, recv_sem_of):
@@ -158,33 +177,43 @@
 
             sends.append((remote, is_self))
 
-    gather_pairs = (
-        (pick, rows_out.at[:, row_me, col_me]),
-        (wcot, cotr_out.at[:, row_me, col_me]),
-        (counts, cnt_in.at[at_me]),
-    )
     for step in range(n_shard):
         t = (s + step) % n_shard
+        which, c = t // cuts, t % cuts
         send_to(
             {"dp": owner, "shard": t},
             jnp.logical_and(owner == d, t == s),
-            gather_pairs,
-            lambda i: g_send.at[i, step],
-            lambda i: g_recv.at[i, at_me],
+            (
+                (pick.at[which, :, cut_cols(0, c)], full.at[which, row_me, cut_cols(k_me, c)]),
+                (cnt, cnt_in.at[at_me]),
+            ),
+            lambda i: (g_send, c_send)[i].at[step],
+            lambda i: (g_recv, c_recv)[i].at[at_me],
         )
-    for e in range(n_dp):
-        for k in range(per):
-            at = e * per + k
-            r = pl.ds(e * slots, slots)
-            c = pl.ds(k * feats, feats)
-            for i, dst in enumerate(
-                (rows_out.at[:, r, c], cotr_out.at[:, r, c], cnt_in.at[at])
-            ):
-                pltpu.make_async_copy(dst, dst, g_recv.at[i, at]).wait()
+    spread = []
+    for k in range(per):
+        own = full.at[s // cuts, :, cut_cols(k, s % cuts)]
+        for e in range(n_dp):
+            got = full.at[s // cuts, pl.ds(e * slots, slots), cut_cols(k, s % cuts)]
+            pltpu.make_async_copy(got, got, g_recv.at[e * per + k]).wait()
+        for step in range(1, n_shard):
+            copy = pltpu.make_async_remote_copy(
+                src_ref=own, dst_ref=own, send_sem=b_send.at[k, step], recv_sem=b_recv.at[k, s],
+                device_id={"dp": d, "shard": (s + step) % n_shard}, device_id_type=MESH,
+            )
+            copy.start()
+            spread.append(copy)
+    for at in range(n_dp * per):
+        pltpu.make_async_copy(cnt_in.at[at], cnt_in.at[at], c_recv.at[at]).wait()
+    for k in range(per):
+        for step in range(1, n_shard):
+            t = (s + step) % n_shard
+            got = full.at[t // cuts, :, cut_cols(k, t % cuts)]
+            pltpu.make_async_copy(got, got, b_recv.at[k, t]).wait()
     total = cnt_in[0]
     for e in range(1, n_dp):
         total = total + cnt_in[e * per]
-    tot_out[...] = total
+    tot_out[...] = 1.0 / jnp.maximum(total, 1).astype(jnp.float32)
 
     stages = [(e, j) for e in range(experts) for j in range(PIECES)]
 
@@ -192,11 +221,11 @@
         return pl.ds(pl.multiple_of(who * half + j * piece, 128), piece)
 
     def partials(e, cols):
-        rows = rows_out[e]
+        rows = full[e]
         gate = jnp.dot(rows, gate_w[e, :, cols], preferred_element_type=jnp.float32)
         up = jnp.dot(rows, up_w[e, :, cols], preferred_element_type=jnp.float32)
         down = lax.dot_general(
-            cotr_out[e], down_w[e, cols, :], (((1,), (1,)), ((), ())),
+            full[experts + e], down_w[e, cols, :], (((1,), (1,)), ((), ())),
             preferred_element_type=jnp.float32,
         )
         return gate, up, down
@@ -291,28 +320,31 @@
         if t >= 2:
             finish(t - 2)
     add_pair(last - 1)
+    for e in range(experts):
+        rows_out[e] = full[e]
+        cotr_out[e] = full[experts + e]
     finish(last - 2)
     for e in range(experts - 1):
         backward(e)
     finish(last - 1)
     backward(experts - 1)
 
-    choose_back = (
-        slot_row[...] == lax.broadcasted_iota(jnp.int32, (tokens.shape[0], experts * slots), 0)
-    ).astype(jnp.float32)
-    sums = []
+    result = jnp.zeros(tokens.shape, jnp.float32)
+    places = lax.broadcasted_iota(jnp.int32, (count, slots), 0)
     for e in range(experts):
         for t in range(n_shard):
             pltpu.make_async_copy(parts.at[e, t], parts.at[e, t], r_recv.at[e, t]).wait()
         acc = parts[e, 0].astype(jnp.float32)
         for t in range(1, n_shard):
             acc = acc + parts[e, t].astype(jnp.float32)
-        sums.append(acc)
-    tok_out[...] = jnp.dot(
-        choose_back, jnp.concatenate(sums, axis=0),
-        preferred_element_type=jnp.float32, precision=lax.Precision.HIGHEST,
-    ).astype(jnp.bfloat16)
-
+        chosen = (slot_ids[e : e + 1, :] == places).astype(jnp.float32)
+        result = result + jnp.dot(
+            chosen, acc, preferred_element_type=jnp.float32, precision=lax.Precision.HIGHEST
+        )
+    tok_out[...] = result.astype(jnp.bfloat16)
+
+    for copy in spread:
+        copy.wait_send()
     for t in range(last):
         pair_copy(t).wait_send()
         across_copy(t).wait_send()
@@ -323,6 +355,54 @@
         @pl.when(jnp.logical_not(is_self))
         def _():
             remote.wait_send()
+
+
+def outer_kernel(rows, cots, hidden, gate, up, scale, gate_out, up_out, down_out):
+    e = pl.program_id(0)
+    factor = scale[pl.ds(e, 1), :][:, :1]
+
+    def fill(left, right, out):
+        wide = right.shape[2]
+        step = 256 if wide % 256 == 0 else wide
+        for b in range(wide // step):
+            c = pl.ds(b * step, step)
+            value = lax.dot_general(
+                left[0], right[0, :, c], (((0,), (0,)), ((), ())),
+                preferred_element_type=jnp.float32,
+            )
+            out[0, :, c] = (value * factor).astype(jnp.bfloat16)
+
+    fill(rows, gate, gate_out)
+    fill(rows, up, up_out)
+    fill(hidden, cots, down_out)
+
+
+def weight_grads(rows, cots, hidden, gate, up, scale):
+    experts, routed, depth = rows.shape
+    width = hidden.shape[2]
+    blocks = 4
+    tall, long = depth // blocks, width // blocks
+    bf16 = jnp.bfloat16
+    whole = lambda n: pl.BlockSpec((1, routed, n), lambda e, b: (e, 0, 0))
+    part = lambda n: pl.BlockSpec((1, routed, n), lambda e, b: (e, 0, b))
+    wide_out = pl.BlockSpec((1, tall, width), lambda e, b: (e, b, 0))
+    down_out = pl.BlockSpec((1, long, depth), lambda e, b: (e, b, 0))
+    return pl.pallas_call(
+        outer_kernel,
+        grid=(experts, blocks),
+        out_shape=(
+            jax.ShapeDtypeStruct((experts, depth, width), bf16),
+            jax.ShapeDtypeStruct((experts, depth, width), bf16),
+            jax.ShapeDtypeStruct((experts, width, depth), bf16),
+        ),
+        in_specs=[
+            part(tall), whole(depth), part(long), whole(width), whole(width),
+            pl.BlockSpec(scale.shape, lambda e, b: (0, 0)),
+        ],
+        out_specs=(wide_out, wide_out, down_out),
+        compiler_params=pltpu.CompilerParams(vmem_limit_bytes=62 * 1024 * 1024),
+        name="weight_grads",
+    )(rows, cots, hidden, gate, up, scale)
 
 
 def on_device_fused(
@@ -334,12 +414,6 @@
     feats = tokens.shape[1]
     routed = slots * n_dp
     per = n_shard // n_dp
-    position = lax.broadcasted_iota(jnp.int32, slot_tokens.shape, 1)
-    alive_mask = (position < live_counts).astype(jnp.float32)
-    scale_col = (gate_weights * alive_mask).reshape(-1, 1)
-    counts = jnp.broadcast_to(
-        jnp.pad(live_counts, ((0, 8 - experts), (0, 0))), (8, 128)
-    ).astype(jnp.int32)
     stages = experts * PIECES
     piece = width // 2 // PIECES
     vmem = pl.BlockSpec(memory_space=pltpu.VMEM)
@@ -355,23 +429,25 @@
             jax.ShapeDtypeStruct((experts, routed, width), bf16),
             jax.ShapeDtypeStruct((experts, routed, width), bf16),
             jax.ShapeDtypeStruct((experts, routed, width), bf16),
-            jax.ShapeDtypeStruct((8, 128), jnp.int32),
+            jax.ShapeDtypeStruct((8, 128), jnp.float32),
             jax.ShapeDtypeStruct(tokens.shape, bf16),
         ),
-        in_specs=[vmem] * 6 + [hbm] * 3,
+        in_specs=[vmem] * 5 + [hbm] * 3,
         out_specs=(vmem,) * 7,
         scratch_shapes=[
             pltpu.VMEM((experts, depth, width), bf16),
             pltpu.VMEM((experts, depth, width), bf16),
             pltpu.VMEM((experts, width, depth), bf16),
-            pltpu.VMEM((experts, slots, feats), bf16),
-            pltpu.VMEM((experts, slots, feats), bf16),
+            pltpu.VMEM((2 * experts, slots, feats), bf16),
+            pltpu.VMEM((2 * experts, routed, depth), bf16),
             block, block, block, block, block,
             pltpu.VMEM((experts, routed, depth), bf16),
             pltpu.VMEM((experts, n_shard, slots, feats), bf16),
+            pltpu.VMEM((8, 128), jnp.int32),
             pltpu.VMEM((n_dp * per, 8, 128), jnp.int32),
             dma((3, experts)),
-            dma((3, n_shard)), dma((3, n_dp * per)),
+            dma((n_shard,)), dma((n_dp * per,)), dma((n_shard,)), dma((n_dp * per,)),
+            dma((per, n_shard)), dma((per, n_shard)),
             dma((stages,)), dma((stages,)), dma((stages,)), dma((stages,)),
             dma((3, stages)), dma((3, stages)),
             dma((experts, n_dp * per)), dma((experts, n_shard)),
@@ -381,30 +457,20 @@
         ),
         name="route_step",
     )(
-        slot_tokens.reshape(-1, 1), slot_tokens.reshape(1, -1), scale_col, counts,
-        tokens, cotangent, gate_proj, up_proj, down_proj,
-    )
-    block_rows, block_cot, hidden_all, gate_all, up_all, totals, grad_tokens = outs
-    scale_back = totals[:experts, :1].astype(jnp.float32)[:, :, None]
-    grad_down_proj = (
-        jnp.einsum("erf,erd->efd", hidden_all, block_cot, preferred_element_type=jnp.float32)
-        / scale_back
-    ).astype(jnp.bfloat16)
-    grad_gate_proj = (
-        jnp.einsum("erd,erf->edf", block_rows, gate_all, preferred_element_type=jnp.float32)
-        / scale_back
-    ).astype(jnp.bfloat16)
-    grad_up_proj = (
-        jnp.einsum("erd,erf->edf", block_rows, up_all, preferred_element_type=jnp.float32)
-        / scale_back
-    ).astype(jnp.bfloat16)
-    return (grad_tokens, grad_gate_proj, grad_up_proj, grad_down_proj)
+        slot_tokens, gate_weights, live_counts, tokens, cotangent, gate_proj, up_proj, down_proj,
+    )
+    block_rows, block_cot, hidden_all, gate_all, up_all, scale, grad_tokens = outs
+    grads = weight_grads(block_rows, block_cot, hidden_all, gate_all, up_all, scale)
+    return (grad_tokens, *grads)
 
 
 def pick_form(n_dp, n_shard, *args):
-    feats = args[0].shape[1]
-    aligned = feats % 128 == 0 and args[2].shape[2] % (256 * PIECES) == 0
-    if n_dp == 4 and n_shard % n_dp == 0 and aligned and args[5].shape[1] % 16 == 0:
+    feats, experts = args[0].shape[1], args[2].shape[0]
+    depth, width = args[2].shape[1:]
+    cuts = n_shard // (2 * experts)
+    even = n_dp == 4 and n_shard % n_dp == 0 and n_shard == 2 * experts * cuts
+    aligned = even and experts <= 8 and feats % (128 * cuts) == 0 and depth % 512 == 0
+    if aligned and width % (256 * PIECES) == 0 and width % 512 == 0 and args[5].shape[1] % 16 == 0:
         return on_device_fused(n_dp, n_shard, *args)
     return on_device(*args)
 

time: 99 us -> 90.8 us (0.917)
  matrix products: 23.2 us -> 0 us
  Pallas kernels: 68 us -> 87.1 us
  local copies, waits for them, and re-layouts: 5.31 us -> 2.84 us
  other arithmetic: 1.55 us -> 0 us
    dot_general x3 -> x0, matrix products: 23.2 us -> none  [the longest x1 9.78 us: on_device_fused(): jnp.einsum('erf,erd->efd', hidden_all, block_cot, preferred_element_type=...]
    pallas_call x0 -> x1, Pallas kernels: none -> 15.9 us  [weight_grads(): pl.pallas_call(outer_kernel, grid=(experts, blocks), out_shape=(jax.Shape...]
    reshape x3 -> x0, local copies, waits for them, and re-layouts: 3.34 us -> none  [the longest x1 1.37 us: on_device_fused(): slot_tokens.reshape(-1, 1)]
    pallas_call x1, Pallas kernels: 68 us -> 71.2 us  [on_device_fused(): pl.pallas_call(functools.partial(step_kernel, n_dp, n_shard), out_shape=(...]
    unnamed x9 -> x2, local copies, waits for them, and re-layouts: 0.66 us -> 2.84 us
    broadcast_in_dim x2 -> x0, local copies, waits for them, and re-layouts: 1.32 us -> none  [on_device_fused(): jnp.broadcast_to(jnp.pad(live_counts, ((0, 8 - experts), (0, 0))), (8, 128))]
where the time goes in v2:
time: 90.8 us; the launch traced here: 90.5 us
  Pallas kernels  87.1 us (96%)
  local copies, waits for them, and re-layouts  2.84 us (3%)
    pallas_call x1, Pallas kernels, on_device_fused(): pl.pallas_call(functools.partial(step_kernel, n_dp, n_shard), out_shape=(...  71.2 us
    pallas_call x1, Pallas kernels, weight_grads(): pl.pallas_call(outer_kernel, grid=(experts, blocks), out_shape=(jax.Shape...  15.9 us
    unnamed x2, local copies, waits for them, and re-layouts  2.84 us

profile of v2, /device:TPU:3, one launch (start us, length us, event | category | flops | bytes accessed | tf_op | source)
XLA Modules:
  0.0 90.5 jit_solution(8274681378356852295)
XLA Ops:
  0.6 1.3 %copy.12.live = s32[2,1]{1,0:T(2,128)} copy(s32[2,1]{0,1:T(1,128)} %param.15) | data formatting | bytes 16 | tf_op args[7]
  1.9 71.2 %route_step.1 = (bf16[2,64,1536]{2,1,0:T(8,128)(2,1)}, bf16[2,64,1536]{2,1,0:T(8,128)(2,1)}, bf16[2,64,2048]{2,1,0:T(8,128)(2,1)}, bf16[2,64,2048]{2,1,0:T(8,128...) custom-call(s32[2,16]{1,0:T(2,128)} %slot_ids.1, f32[2,16]{1,0:T(2,128)} %weights.1, ...), custom_call_target="tpu_custom_call" | custom-call | tf_op jit(solution)/shard_map/route_step/pallas_call | solution.py:424
  73.1 15.9 %weight_grads.1 = (bf16[2,1536,2048]{2,1,0:T(8,128)(2,1)}, bf16[2,1536,2048]{2,1,0:T(8,128)(2,1)}, bf16[2,2048,1536]{2,1,0:T(8,128)(2,1)}) custom-call(bf16[2,64,1536]{2,1,0:T(8,128)(2,1)} %get-tuple-element.15.rows, bf16[2,64,1536]{2,1,0:T(8,128)(2,1)} %get-tuple-element.16.cots, bf16[2,64,2048]{2,1,0:T(8,128)(2,1)} %get-tuple-element.17.hidden, ...), custom_call_target="tpu_custom_call" | custom-call | tf_op jit(solution)/shard_map/weight_grads/pallas_call | solution.py:390
  89.0 1.5 %copy.14 = bf16[64,768]{1,0:T(8,128)(2,1)} copy(bf16[64,768]{1,0:T(8,128)(2,1)} %get-tuple-element.28) | data formatting | bytes 196608

commit v3 on v2

--- a/solution.py
+++ b/solution.py
@@ -191,25 +191,38 @@
             lambda i: (g_recv, c_recv)[i].at[at_me],
         )
     spread = []
+    side = s + 1 - 2 * (s % 2)
+
+    def share(ref, k, source, lane, target):
+        copy = pltpu.make_async_remote_copy(
+            src_ref=ref, dst_ref=ref, send_sem=b_send.at[k, lane], recv_sem=b_recv.at[k, source],
+            device_id={"dp": d, "shard": target}, device_id_type=MESH,
+        )
+        copy.start()
+        spread.append(copy)
+
+    def arrived(k, t):
+        got = full.at[t // cuts, :, cut_cols(k, t % cuts)]
+        pltpu.make_async_copy(got, got, b_recv.at[k, t]).wait()
+        return got
+
     for k in range(per):
         own = full.at[s // cuts, :, cut_cols(k, s % cuts)]
         for e in range(n_dp):
             got = full.at[s // cuts, pl.ds(e * slots, slots), cut_cols(k, s % cuts)]
             pltpu.make_async_copy(got, got, g_recv.at[e * per + k]).wait()
-        for step in range(1, n_shard):
-            copy = pltpu.make_async_remote_copy(
-                src_ref=own, dst_ref=own, send_sem=b_send.at[k, step], recv_sem=b_recv.at[k, s],
-                device_id={"dp": d, "shard": (s + step) % n_shard}, device_id_type=MESH,
-            )
-            copy.start()
-            spread.append(copy)
+        share(own, k, s, 0, side)
+        for step in range(1, n_shard // 2):
+            share(own, k, s, step, (s + 2 * step) % n_shard)
     for at in range(n_dp * per):
         pltpu.make_async_copy(cnt_in.at[at], cnt_in.at[at], c_recv.at[at]).wait()
-    for k in range(per):
-        for step in range(1, n_shard):
-            t = (s + step) % n_shard
-            got = full.at[t // cuts, :, cut_cols(k, t % cuts)]
-            pltpu.make_async_copy(got, got, b_recv.at[k, t]).wait()
+    for step in range(1, n_shard // 2):
+        t = (s + 2 * step) % n_shard
+        for k in range(per):
+            share(arrived(k, t), k, t, n_shard // 2 + step, side)
+    for step in range(n_shard // 2):
+        for k in range(per):
+            arrived(k, (side + 2 * step) % n_shard)
     total = cnt_in[0]
     for e in range(1, n_dp):
         total = total + cnt_in[e * per]

time: 90.8 us -> 87.6 us (0.965)
  Pallas kernels: 87.1 us -> 83.2 us
    pallas_call x1, Pallas kernels: 71.2 us -> 67.3 us  [on_device_fused(): pl.pallas_call(functools.partial(step_kernel, n_dp, n_shard), out_shape=(...]
where the time goes in v3:
time: 87.6 us; the launch traced here: 86.7 us
  Pallas kernels  83.2 us (95%)
  local copies, waits for them, and re-layouts  2.84 us (3%)
    pallas_call x1, Pallas kernels, on_device_fused(): pl.pallas_call(functools.partial(step_kernel, n_dp, n_shard), out_shape=(...  67.3 us
    pallas_call x1, Pallas kernels, weight_grads(): pl.pallas_call(outer_kernel, grid=(experts, blocks), out_shape=(jax.Shape...  15.9 us
    unnamed x2, local copies, waits for them, and re-layouts  2.84 us

profile of v3, /device:TPU:3, one launch (start us, length us, event | category | flops | bytes accessed | tf_op | source)
XLA Modules:
  0.0 86.7 jit_solution(5458163512723408821)
XLA Ops:
  0.6 1.3 %copy.12.live = s32[2,1]{1,0:T(2,128)} copy(s32[2,1]{0,1:T(1,128)} %param.15) | data formatting | bytes 16 | tf_op args[7]
  1.9 67.3 %route_step.1 = (bf16[2,64,1536]{2,1,0:T(8,128)(2,1)}, bf16[2,64,1536]{2,1,0:T(8,128)(2,1)}, bf16[2,64,2048]{2,1,0:T(8,128)(2,1)}, bf16[2,64,2048]{2,1,0:T(8,128...) custom-call(s32[2,16]{1,0:T(2,128)} %slot_ids.1, f32[2,16]{1,0:T(2,128)} %weights.1, ...), custom_call_target="tpu_custom_call" | custom-call | tf_op jit(solution)/shard_map/route_step/pallas_call | solution.py:437
  69.3 15.9 %weight_grads.1 = (bf16[2,1536,2048]{2,1,0:T(8,128)(2,1)}, bf16[2,1536,2048]{2,1,0:T(8,128)(2,1)}, bf16[2,2048,1536]{2,1,0:T(8,128)(2,1)}) custom-call(bf16[2,64,1536]{2,1,0:T(8,128)(2,1)} %get-tuple-element.15.rows, bf16[2,64,1536]{2,1,0:T(8,128)(2,1)} %get-tuple-element.16.cots, bf16[2,64,2048]{2,1,0:T(8,128)(2,1)} %get-tuple-element.17.hidden, ...), custom_call_target="tpu_custom_call" | custom-call | tf_op jit(solution)/shard_map/weight_grads/pallas_call | solution.py:403
  85.1 1.5 %copy.14 = bf16[64,768]{1,0:T(8,128)(2,1)} copy(bf16[64,768]{1,0:T(8,128)(2,1)} %get-tuple-element.28) | data formatting | bytes 196608
